TPU v7x, 32 devices: a whole 2x2x4 slice. The times are simulated.
32 devices in a mesh: ens: 2 (over y), wave: 4 (over z), lev: 2 (over x), pot: 2 (over core).
Axes of the slice: x: 2, y: 2, z: 4, core: 2. Of those that a mesh axis runs over, the one named last changes fastest.
Arguments:
- spectra: bfloat16 [4, 64, 2, 64, 512], P(('ens', 'pot'), 'wave', None, 'lev'), parts along dimension 0, may hold values from -0.1875 to 0.1875
- legendre: bfloat16 [64, 768, 512], P('wave', 'lev'), may hold values from -0.25 to 0.25
- row_map: int32 [4, 32], replicated, may hold values from 0 to 767, as said below
- seg_map: int32 [4, 32], replicated, may hold values from 0 to 11
- interp: bfloat16 [4, 32, 128, 128], P('wave'), may hold values from -0.5 to 0.5
- edges: int32 [4, 4, 12288], P('wave'), may hold values from 0 to 4351, as said below
- inv_len: float32 [4, 2, 12288], P('wave'), may hold values from 0.5 to 2
Outputs:
- normal_wind: bfloat16 [128, 49152], P(('ens', 'lev', 'pot'), 'wave'), parts along dimension 0
There are 2 independent parts, one for each index of `ens`. A program takes and returns all parts, laid end to end along the dimension named above; an argument that names none is the same for every part. Nothing has to cross between parts.
Inputs may be any that keep to these rules, and one draw needn't show every extreme that they name: For each patch q and each band b of rows b * 192 to b * 192 + 191, at most 24 entries of row_map[q, :] lie in band b, and every patch has exactly 24 entries in some band. edges[q, 0, e] lies in 128 to 4223, and edges[q, 1, e], edges[q, 2, e], edges[q, 3, e] each lie within 128 of it.
All inputs are finite; a program needn't handle non-finite values.
Results may differ from a plain program's by a relative error of at most 0.0068.
Values may be sent and summed in bfloat16 or wider, within the bound.
No kernel may reach another device: no remote copies, remote signals or barrier semaphores. Data moves between devices by JAX's collectives and lax.ppermute only.
A program may use at most 128 MiB of HBM per device.

v0:
```python
import math
import jax
import jax.numpy as jnp
from jax import lax
from jax.sharding import PartitionSpec as P

NLON = 1536
BLOCK = 128
HALO = 128


def extended_2(cells, sides, width):
    for axis, dim in sides:
        count = lax.axis_size(axis)
        head = lax.slice_in_dim(cells, 0, width, axis=dim)
        tail = lax.slice_in_dim(cells, cells.shape[dim] - width, cells.shape[dim], axis=dim)
        cells = jnp.concatenate(
            [
                lax.ppermute(tail, axis, [(i, (i + 1) % count) for i in range(count)]),
                cells,
                lax.ppermute(head, axis, [((i + 1) % count, i) for i in range(count)]),
            ],
            axis=dim,
        )
    return cells


def fourier_matrix(wave_count, longitude_count):
    wave_index = lax.broadcasted_iota(jnp.int32, (wave_count, longitude_count), 0)
    lon_index = lax.broadcasted_iota(jnp.int32, (wave_count, longitude_count), 1)
    angle_values = (wave_index * lon_index % longitude_count).astype(jnp.float32) * (
        2.0 * math.pi / longitude_count
    )
    factor = jnp.where(wave_index == 0, 1.0, 2.0).astype(jnp.float32)
    return jnp.stack(
        [factor * jnp.cos(angle_values), -factor * jnp.sin(angle_values)], axis=0
    ).astype(jnp.bfloat16)


def body(spectra, legendre, row_map, seg_map, interp, edges, inv_len):
    own_spectra = spectra[0]
    spectral = jnp.einsum(
        "mrj,mclj->lrcm",
        legendre,
        lax.all_gather(own_spectra, "lev", axis=2, tiled=True),
        preferred_element_type=jnp.float32,
    ).astype(jnp.bfloat16)
    banded = lax.all_to_all(
        lax.all_to_all(spectral, "lev", split_axis=0, concat_axis=1, tiled=True),
        "wave",
        split_axis=1,
        concat_axis=3,
        tiled=True,
    )
    fourier_modes = fourier_matrix(banded.shape[3], NLON)
    grid_field = jnp.einsum(
        "lrcm,cmk->lrk", banded, fourier_modes, preferred_element_type=jnp.float32
    ).astype(jnp.bfloat16)
    level_count = grid_field.shape[0]
    rows_dev = grid_field.shape[1]
    segments = NLON // BLOCK
    blocks_dev = row_map.shape[1]
    patch_count = lax.axis_size("wave")
    capacity = min(blocks_dev, max(3, 3 * blocks_dev // patch_count))
    own_band = lax.axis_index("wave")
    row_band = row_map // rows_dev
    is_mine = (row_band == own_band).astype(jnp.int32)
    slot_rank = jnp.cumsum(is_mine, axis=1) - is_mine
    slot_ids = jnp.arange(capacity, dtype=jnp.int32)
    slot_hit = (is_mine[:, :, None] == 1) & (slot_rank[:, :, None] == slot_ids[None, None, :])
    piece_index = row_map % rows_dev * segments + seg_map
    source_index = jnp.sum(jnp.where(slot_hit, piece_index[:, :, None], 0), axis=1)
    pieces = grid_field.reshape(level_count, rows_dev * segments, BLOCK)
    outgoing = jnp.take(pieces, source_index.reshape(-1), axis=1)
    incoming = lax.all_to_all(outgoing, "wave", split_axis=1, concat_axis=1, tiled=True)
    own_rows = lax.dynamic_index_in_dim(row_map, own_band, 0, keepdims=False)
    own_row_band = own_rows // rows_dev
    block_ids = jnp.arange(blocks_dev, dtype=jnp.int32)
    same_band = own_row_band[:, None] == own_row_band[None, :]
    earlier = block_ids[None, :] < block_ids[:, None]
    own_rank = jnp.sum((same_band & earlier).astype(jnp.int32), axis=1)
    arrival = own_row_band * capacity + own_rank
    gathered = jnp.take(incoming, arrival, axis=1)
    cell_field = jnp.einsum(
        "kij,lkj->lki", interp[0], gathered, preferred_element_type=jnp.float32
    ).astype(jnp.bfloat16)
    cell_field = cell_field.reshape(level_count, blocks_dev * BLOCK)
    extended = extended_2(cell_field, (("wave", 1),), HALO)
    edge_ids = edges[0]
    lengths = inv_len[0]
    pot_index = lax.axis_index("pot")
    first_cell = jnp.where(pot_index == 0, edge_ids[2], edge_ids[0])
    second_cell = jnp.where(pot_index == 0, edge_ids[3], edge_ids[1])
    weights_edge = jnp.where(pot_index == 0, -lengths[1], lengths[0])
    edge_term = (
        jnp.take(extended, second_cell, axis=1).astype(jnp.float32)
        - jnp.take(extended, first_cell, axis=1).astype(jnp.float32)
    ) * weights_edge
    normal_wind = lax.psum_scatter(edge_term, "pot", scatter_dimension=0, tiled=True).astype(
        jnp.bfloat16
    )
    return normal_wind


def solution(mesh):
    return jax.shard_map(
        body,
        mesh=mesh,
        in_specs=(
            P(("ens", "pot"), "wave", None, "lev", None),
            P("wave", "lev", None),
            P(),
            P(),
            P("wave", None, None, None),
            P("wave", None, None),
            P("wave", None, None),
        ),
        out_specs=P(("ens", "lev", "pot"), "wave"),
        check_vma=False,
    )
```

profile of v0, /device:TPU:0, one launch (start us, length us, event | category | flops | bytes accessed | tf_op | source)
XLA Modules:
  0.0 373.4 jit_solution(1620999810213235277)
XLA Ops:
  6.5 0.7 all-gather.3.cloned.1.call-update
  7.3 0.7 fusion.31
  9.3 0.7 bitcast_select_fusion.1
  10.2 2.2 broadcast_select_fusion.2
  12.3 32.4 %all-gather.3.cloned.1.call-done = bf16[1,16,2,64,512]{4,3,2,1,0:T(8,128)(2,1)} async-done(((bf16[1,16,2,32,512]{4,3,2,1,0:T(8,128)(2,1)}), bf16[1,16,2,64,512]{4,3,2,1,0:T(8,128)(2,1)}) %all-gather.3.cloned.1.call-update) | async-done | bytes 2097168 | tf_op jit(solution)/shard_map/all_gather | solution.py:45
  44.7 5.4 %fusion.8 = bf16[64,384,2,16]{1,0,2,3:T(8,128)(2,1)S(1)} fusion(bf16[16,384,512]{2,1,0:T(8,128)(2,1)} %param.10, bf16[1,16,2,64,512]{4,3,2,1,0:T(8,128)(2,1)} %all-gather.3.cloned.1.call-done), kind=kOutput, calls=%fused_computation.10 | convolution fusion | flops 806092800 | bytes 9961472 | tf_op jit(solution)/shard_map/mrj,mclj->lrcm/dot_general | solution.py:42
  50.1 2.8 copy.47
  52.9 3.7 all-to-all-start
  56.6 1.7 multiply_convert_fusion
  58.3 17.6 %all-to-all-done = bf16[64,384,2,16]{1,2,3,0:T(2,128)(2,1)S(1)} async-done(((bf16[64,384,2,16]{1,2,3,0:T(2,128)(2,1)}), bf16[64,384,2,16]{1,2,3,0:T(2,128)(2,1)S(1)}, u32[]{:S(2)}, u32[]{:S(2)}) %all-to-all-start) | async-done | bytes 1572896 | tf_op jit(solution)/shard_map/all_to_all | solution.py:49
  75.9 8.6 %copy.59 = bf16[32,2,384,2,16]{0,4,3,2,1:T(8,128)(2,1)} copy(bf16[32,2,384,2,16]{2,3,4,0,1:T(2,128)(2,1)S(1)} %bitcast.87) | data formatting | bytes 3145728 | tf_op jit(solution)/shard_map/all_to_all | solution.py:49
  84.5 8.3 %reshape.312 = bf16[4,2,98304]{2,1,0:T(2,128)(2,1)} reshape(bf16[768,2,16,32]{3,2,1,0:T(8,128)(2,1)} %bitcast.83) | data formatting | bytes 3145728
  92.8 4.7 %all-to-all-start.1 = ((bf16[4,2,98304]{2,1,0:T(2,128)(2,1)}), bf16[4,2,98304]{2,1,0:T(2,128)(2,1)S(1)}, u32[]{:S(2)}, u32[]{:S(2)}) async-start(bf16[4,2,98304]{2,1,0:T(2,128)(2,1)} %reshape.312), calls=%async_computation.1 | async-start | bytes 3145728 | tf_op jit(solution)/shard_map/all_to_all | solution.py:48
  98.2 35.2 %all-to-all-done.1 = bf16[4,2,98304]{2,1,0:T(2,128)(2,1)S(1)} async-done(((bf16[4,2,98304]{2,1,0:T(2,128)(2,1)}), bf16[4,2,98304]{2,1,0:T(2,128)(2,1)S(1)}, u32[]{:S(2)}, u32[]{:S(2)}) %all-to-all-start.1) | async-done | bytes 1572896 | tf_op jit(solution)/shard_map/all_to_all | solution.py:48
  133.5 4.6 %reshape.313 = bf16[768,2,16,32]{3,2,1,0:T(8,128)(2,1)} reshape(bf16[4,2,98304]{2,1,0:T(2,128)(2,1)S(1)} %all-to-all-done.1) | data formatting | bytes 3145728
  138.1 10.1 %copy.60 = bf16[32,4,192,2,16]{2,1,4,3,0:T(4,128)(2,1)S(1)} copy(bf16[32,4,192,2,16]{0,4,3,2,1:T(8,128)(2,1)} %bitcast.84) | data formatting | bytes 3145728 | tf_op jit(solution)/shard_map/all_to_all | solution.py:48
  148.7 9.1 %bitcast_convert_fusion = bf16[32,192,1536]{2,1,0:T(8,128)(2,1)} fusion(bf16[32,192,2,64]{1,3,2,0:T(8,128)(2,1)S(1)} %bitcast.85, bf16[1,64,1536]{2,1,0:T(8,128)(2,1)S(1)} %get-tuple-element.15, bf16[1,64,1536]{2,1,0:T(8,128)(2,1)S(1)} %get-tuple-element.16), kind=kOutput, calls=%fused_computation.4 | convolution fusion | flops 2425552896 | bytes 20840448 | tf_op jit(solution)/shard_map/lrcm,cmk->lrk/dot_general | solution.py:56
  157.8 35.2 %reshape.265 = bf16[32,2304,128]{2,1,0:T(8,128)(2,1)} reshape(bf16[32,192,1536]{2,1,0:T(8,128)(2,1)} %bitcast_convert_fusion) | data formatting | bytes 37748736 | tf_op jit(solution)/shard_map/reshape | solution.py:73
  193.0 20.7 %copy.52 = bf16[32,2304,128]{2,0,1:T(8,128)(2,1)} copy(bf16[32,2304,128]{2,1,0:T(8,128)(2,1)} %reshape.265) | data formatting | bytes 37748736 | tf_op jit(solution)/shard_map/reshape | solution.py:73
  213.7 7.1 %gather_fusion = bf16[96,32,128]{2,1,0:T(8,128)(2,1)S(1)} fusion(bf16[32,2304,128]{2,0,1:T(8,128)(2,1)} %copy.52, s32[1024]{0:T(1024)S(1)} %pad_clamp_fusion.1), kind=kCustom, calls=%fused_computation.2 | custom fusion | bytes 1573248 | tf_op jit(solution)/shard_map/jit(_take)/gather | solution.py:74
  220.8 1.1 select_bitcast_fusion
  221.9 3.5 all-to-all-start.2
  225.6 19.5 %all-to-all-done.2 = bf16[32,96,128]{2,0,1:T(8,128)(2,1)S(1)} async-done(((bf16[32,96,128]{2,0,1:T(8,128)(2,1)}), bf16[32,96,128]{2,0,1:T(8,128)(2,1)S(1)}, u32[]{:S(2)}, u32[]{:S(2)}) %all-to-all-start.2) | async-done | bytes 786464 | tf_op jit(solution)/shard_map/all_to_all | solution.py:75
  246.4 1.5 collective-permute-start.1
  248.5 1.6 collective-permute-done.1
  250.1 3.3 collective-permute-done
  253.9 43.3 %gather_fusion.3 = bf16[12288,32]{1,0:T(8,128)(2,1)} fusion(bf16[32,4352]{0,1:T(8,128)(2,1)S(1)} %copy.54, s32[12288]{0:T(1024)S(1)} %fusion.28), kind=kCustom, calls=%fused_computation.1.clone | custom fusion | bytes 1622016 | tf_op jit(solution)/shard_map/jit(_take)/gather | solution.py:97
  297.3 43.3 %gather_fusion.2 = bf16[12288,32]{1,0:T(8,128)(2,1)} fusion(bf16[32,4352]{0,1:T(8,128)(2,1)S(1)} %copy.54, s32[12288]{0:T(1024)S(1)} %fusion.27), kind=kCustom, calls=%fused_computation.clone | custom fusion | bytes 1622016 | tf_op jit(solution)/shard_map/jit(_take)/gather | solution.py:96
  340.5 12.1 %subtract_multiply_fusion = f32[32,12288]{0,1:T(8,128)} fusion(bf16[12288,32]{1,0:T(8,128)(2,1)} %gather_fusion.3, bf16[12288,32]{1,0:T(8,128)(2,1)} %gather_fusion.2, f32[12288]{0:T(1024)S(1)} %bitcast.94, pred[12288]{0:T(1024)(128)(4,1)S(1)} %get-tuple-element.17, pred[12288]{0:T(1024)(128)(4,1)S(1)} %get-tuple-element.18), kind=kLoop, calls=%fused_computation.7 | loop fusion | flops 2359296 | bytes 3219456 | tf_op jit(solution)/shard_map/mul | solution.py:95
  352.6 5.5 %copy.61 = f32[32,12288]{1,0:T(8,128)} copy(f32[32,12288]{0,1:T(8,128)} %subtract_multiply_fusion) | data formatting | bytes 3145728
  358.2 6.4 %reduce-scatter.4.cloned.1.call-done = f32[16,12288]{1,0:T(8,128)} async-done(((f32[32,12288]{1,0:T(8,128)}), f32[16,12288]{1,0:T(8,128)}) %reduce-scatter.4.cloned.1.call-update) | async-done | bytes 786448 | tf_op jit(solution)/shard_map/reduce_scatter | solution.py:99
  364.6 1.9 convert_element_type.57
  (45 shorter events, 5.2 us)
Async XLA Ops:
  6.5 239.1 %copy-start = (bf16[1,32,128,128]{3,2,1,0:T(8,128)(2,1)S(1)}, bf16[1,32,128,128]{3,2,1,0:T(8,128)(2,1)}, u32[]{:S(2)}) copy-start(bf16[1,32,128,128]{3,2,1,0:T(8,128)(2,1)} %param.13) | copy-start | bytes 3145732
  6.5 38.2 %all-gather.3.cloned.1.call-start = ((), (), s32[]{:S(2)}) async-start(), calls=%async_computation.4 | async-start | bytes 3145728 | tf_op jit(solution)/shard_map/all_gather | solution.py:45
  10.2 46.4 %copy-start.5 = (s32[32]{0:T(128)}, s32[32]{0:T(128)S(1)}, u32[]{:S(2)}) copy-start(s32[32]{0:T(128)S(1)} %convert_reduce_fusion) | copy-start | bytes 388
  52.9 23.0 %all-to-all-start = ((bf16[64,384,2,16]{1,2,3,0:T(2,128)(2,1)}), bf16[64,384,2,16]{1,2,3,0:T(2,128)(2,1)S(1)}, u32[]{:S(2)}, u32[]{:S(2)}) async-start(bf16[64,384,2,16]{1,2,3,0:T(2,128)(2,1)} %copy.47), calls=%async_computation | async-start | bytes 3145728 | tf_op jit(solution)/shard_map/all_to_all | solution.py:49
  92.8 4.7 %copy-start.4 = (f32[1,2,12288]{2,1,0:T(2,128)S(1)}, f32[1,2,12288]{2,1,0:T(2,128)}, u32[]{:S(2)}) copy-start(f32[1,2,12288]{2,1,0:T(2,128)} %param.15) | copy-start | bytes 294916
  92.8 40.7 %all-to-all-start.1 = ((bf16[4,2,98304]{2,1,0:T(2,128)(2,1)}), bf16[4,2,98304]{2,1,0:T(2,128)(2,1)S(1)}, u32[]{:S(2)}, u32[]{:S(2)}) async-start(bf16[4,2,98304]{2,1,0:T(2,128)(2,1)} %reshape.312), calls=%async_computation.1 | async-start | bytes 3145728 | tf_op jit(solution)/shard_map/all_to_all | solution.py:48
  213.7 11.7 %copy-start.6 = (s32[32]{0:T(128)S(1)}, s32[32]{0:T(128)}, u32[]{:S(2)}) copy-start(s32[32]{0:T(128)} %copy-done.5) | copy-start | bytes 388
  213.7 11.8 %copy-start.2 = (s32[1,1,12288]{2,1,0:T(1,128)S(1)}, s32[1,1,12288]{2,1,0:T(1,128)}, u32[]{:S(2)}) copy-start(s32[1,1,12288]{2,1,0:T(1,128)} %get-tuple-element.14) | copy-start | bytes 147460
  213.7 11.8 %copy-start.1 = (s32[1,1,12288]{2,1,0:T(1,128)S(1)}, s32[1,1,12288]{2,1,0:T(1,128)}, u32[]{:S(2)}) copy-start(s32[1,1,12288]{2,1,0:T(1,128)} %get-tuple-element.13) | copy-start | bytes 147460
  221.9 23.1 %all-to-all-start.2 = ((bf16[32,96,128]{2,0,1:T(8,128)(2,1)}), bf16[32,96,128]{2,0,1:T(8,128)(2,1)S(1)}, u32[]{:S(2)}, u32[]{:S(2)}) async-start(bf16[32,96,128]{2,0,1:T(8,128)(2,1)} %select_bitcast_fusion), calls=%async_computation.2 | async-start | bytes 1572864 | tf_op jit(solution)/shard_map/all_to_all | solution.py:75
  225.4 139.2 %reduce-scatter.4.cloned.1.call-start = ((), (), s32[]{:S(2)}) async-start(), calls=%async_computation.5 | async-start | bytes 2359296 | tf_op jit(solution)/shard_map/reduce_scatter | solution.py:99
  246.4 3.7 collective-permute-start.1
  247.9 5.4 %collective-permute-start = (bf16[32,128]{1,0:T(8,128)(2,1)S(1)}, bf16[32,128]{1,0:T(8,128)(2,1)S(1)}, u32[]{:S(2)}, u32[]{:S(2)}) collective-permute-start(bf16[32,128]{1,0:T(8,128)(2,1)S(1)} %get-tuple-element.11), channel_id=1, source_target_pairs={{0,4},{4,8},{8,12},{12,0},{1,5},{5,9},{9,13},{13,1},{2,6},{6,10},{... | collective-permute-start | bytes 24584 | tf_op jit(solution)/shard_map/ppermute | solution.py:19
  297.3 43.3 %copy-start.3 = (f32[1,1,12288]{2,1,0:T(1,128)S(1)}, f32[1,1,12288]{2,1,0:T(1,128)}, u32[]{:S(2)}) copy-start(f32[1,1,12288]{2,1,0:T(1,128)} %broadcast_select_fusion) | copy-start | bytes 147460
Sparse Core Ops, SparseCore 0:
  8.9 35.8 all-gather.2
  358.3 6.2 reduce-scatter.3
where the time goes:
time: 375 us; the launch traced here: 373 us
  local copies, waits for them, and re-layouts  191 us (51%)
  waiting for transfers between devices  117 us (31%)
  other arithmetic  22.4 us (6%)
  matrix products  15.2 us (4%)
  starting transfers between devices  14 us (4%)
  between operations  13.6 us (4%)
    reshape x2, local copies, waits for them, and re-layouts, body(): pieces = grid_field.reshape(level_count, rows_dev * segments, BLOCK)  55.9 us
    gather x1, local copies, waits for them, and re-layouts, body(): jnp.take(extended, first_cell, axis=1).astype(jnp.float32)  43.3 us
    gather x1, local copies, waits for them, and re-layouts, body(): jnp.take(extended, second_cell, axis=1).astype(jnp.float32)  43.3 us
    all_to_all x1, waiting for transfers between devices, body(): lax.all_to_all(lax.all_to_all(spectral, 'lev', split_axis=0, concat_axis=...  35.2 us
    all_gather x1, waiting for transfers between devices, body(): lax.all_gather(own_spectra, 'lev', axis=2, tiled=True)  32.4 us
    all_to_all x1, waiting for transfers between devices, body(): lax.all_to_all(outgoing, 'wave', split_axis=1, concat_axis=1, tiled=True)  19.5 us
    unnamed x17, local copies, waits for them, and re-layouts  18.5 us
    all_to_all x1, waiting for transfers between devices, body(): lax.all_to_all(spectral, 'lev', split_axis=0, concat_axis=1, tiled=True)  17.6 us
  transfers between devices with their start and end apart: 7, of which 7 were waited for; matrix products, arithmetic and copies ran while one was open for 2% of the time, Pallas kernels for 0%

commit v1 on v0

--- a/solution.py
+++ b/solution.py
@@ -7,6 +7,21 @@
 NLON = 1536
 BLOCK = 128
 HALO = 128
+
+
+def work_around(array, axis, dim, make, out_dim):
+    ways, here, lap = (lax.axis_size(axis), lax.axis_index(axis), array.shape[dim])
+    results = []
+    for far in range(ways):
+        arriving = (
+            lax.ppermute(array, axis, [(d, (d + 1) % ways) for d in range(ways)])
+            if far + 1 < ways
+            else array
+        )
+        results.append(make(array, (here - far) % ways * lap))
+        array = arriving
+    line = jnp.concatenate(results[::-1], axis=out_dim)
+    return jnp.roll(line, (here + 1) * results[0].shape[out_dim], axis=out_dim)
 
 
 def extended_2(cells, sides, width):
@@ -39,11 +54,14 @@
 
 def body(spectra, legendre, row_map, seg_map, interp, edges, inv_len):
     own_spectra = spectra[0]
-    spectral = jnp.einsum(
-        "mrj,mclj->lrcm",
-        legendre,
-        lax.all_gather(own_spectra, "lev", axis=2, tiled=True),
-        preferred_element_type=jnp.float32,
+    spectral = work_around(
+        own_spectra,
+        "lev",
+        2,
+        lambda shard, start: jnp.einsum(
+            "mrj,mclj->lrcm", legendre, shard, preferred_element_type=jnp.float32
+        ),
+        0,
     ).astype(jnp.bfloat16)
     banded = lax.all_to_all(
         lax.all_to_all(spectral, "lev", split_axis=0, concat_axis=1, tiled=True),

time: 375 us -> 363 us (0.968)
  waiting for transfers between devices: 117 us -> 94.2 us
  starting transfers between devices: 14 us -> 19 us
    all_gather x1 -> x0, waiting for transfers between devices: 32.4 us -> none  [body(): lax.all_gather(own_spectra, 'lev', axis=2, tiled=True)]
    ppermute x0 -> x1, waiting for transfers between devices: none -> 11.5 us  [work_around(): lax.ppermute(array, axis, [(d, (d + 1) % ways) for d in range(ways)])]
    unnamed x17 -> x19, local copies, waits for them, and re-layouts: 18.5 us -> 18.5 us
  transfers between devices with their start and end apart: 7 -> 7, of which waited for: 7 -> 6; matrix products, arithmetic and copies ran while one was open for 2% -> 4% of each run, Pallas kernels for 0% -> 0%
where the time goes in v1:
time: 363 us; the launch traced here: 361 us
  local copies, waits for them, and re-layouts  192 us (53%)
  waiting for transfers between devices  94.2 us (26%)
  other arithmetic  25.1 us (7%)
  starting transfers between devices  19 us (5%)
  matrix products  17.1 us (5%)
  between operations  13.6 us (4%)
    reshape x2, local copies, waits for them, and re-layouts, body(): pieces = grid_field.reshape(level_count, rows_dev * segments, BLOCK)  55.9 us
    gather x1, local copies, waits for them, and re-layouts, body(): jnp.take(extended, second_cell, axis=1).astype(jnp.float32)  43.6 us
    gather x1, local copies, waits for them, and re-layouts, body(): jnp.take(extended, first_cell, axis=1).astype(jnp.float32)  43.6 us
    all_to_all x1, waiting for transfers between devices, body(): lax.all_to_all(lax.all_to_all(spectral, 'lev', split_axis=0, concat_axis=...  34.6 us
    all_to_all x1, waiting for transfers between devices, body(): lax.all_to_all(outgoing, 'wave', split_axis=1, concat_axis=1, tiled=True)  19.5 us
    unnamed x19, local copies, waits for them, and re-layouts  18.5 us
    all_to_all x1, waiting for transfers between devices, body(): lax.all_to_all(spectral, 'lev', split_axis=0, concat_axis=1, tiled=True)  17.3 us
    mul x1, other arithmetic, body(): (jnp.take(extended, second_cell, axis=1).astype(jnp.float32) - jnp.take(e...  12.1 us
  transfers between devices with their start and end apart: 7, of which 6 were waited for; matrix products, arithmetic and copies ran while one was open for 4% of the time, Pallas kernels for 0%

profile of v1, /device:TPU:0, one launch (start us, length us, event | category | flops | bytes accessed | tf_op | source)
XLA Modules:
  0.0 361.3 jit_solution(5306546601771904322)
XLA Ops:
  6.5 3.0 collective-permute-start
  12.2 2.2 broadcast_select_fusion.2
  14.5 1.5 multiply_convert_fusion
  16.1 5.3 %fusion.11 = bf16[32,384,2,16]{1,0,2,3:T(8,128)(2,1)S(1)} fusion(bf16[16,384,512]{2,1,0:T(8,128)(2,1)} %param.10, bf16[1,16,2,32,512]{4,3,2,1,0:T(8,128)(2,1)} %param.9), kind=kOutput, calls=%fused_computation.19 | convolution fusion | flops 402653184 | bytes 8126464 | tf_op jit(solution)/shard_map/mrj,mclj->lrcm/dot_general | solution.py:61
  21.4 11.5 %collective-permute-done = bf16[16,2,32,512]{3,2,1,0:T(8,128)(2,1)S(1)} collective-permute-done((bf16[16,2,32,512]{3,2,1,0:T(8,128)(2,1)}, bf16[16,2,32,512]{3,2,1,0:T(8,128)(2,1)S(1)}, u32[]{:S(2)}, u32[]{:S(2)}) %collective-permute-start) | collective-permute-done | bytes 1048608 | tf_op jit(solution)/shard_map/ppermute | solution.py:17
  32.9 2.0 fusion.8
  34.9 1.4 fusion.7
  36.3 2.8 copy.47
  39.1 3.7 %all-to-all-start = ((bf16[64,384,2,16]{1,2,3,0:T(2,128)(2,1)}), bf16[64,384,2,16]{1,2,3,0:T(2,128)(2,1)S(1)}, u32[]{:S(2)}, u32[]{:S(2)}) async-start(bf16[64,384,2,16]{1,2,3,0:T(2,128)(2,1)} %copy.47), calls=%async_computation | async-start | bytes 3145728 | tf_op jit(solution)/shard_map/all_to_all | solution.py:67
  42.8 1.5 multiply_convert_fusion.1
  44.3 17.3 %all-to-all-done = bf16[64,384,2,16]{1,2,3,0:T(2,128)(2,1)S(1)} async-done(((bf16[64,384,2,16]{1,2,3,0:T(2,128)(2,1)}), bf16[64,384,2,16]{1,2,3,0:T(2,128)(2,1)S(1)}, u32[]{:S(2)}, u32[]{:S(2)}) %all-to-all-start) | async-done | bytes 1572896 | tf_op jit(solution)/shard_map/all_to_all | solution.py:67
  61.6 8.7 %copy.59 = bf16[32,2,384,2,16]{0,4,3,2,1:T(8,128)(2,1)} copy(bf16[32,2,384,2,16]{2,3,4,0,1:T(2,128)(2,1)S(1)} %bitcast.88) | data formatting | bytes 3145728 | tf_op jit(solution)/shard_map/all_to_all | solution.py:67
  70.3 8.3 %reshape.311 = bf16[4,2,98304]{2,1,0:T(2,128)(2,1)} reshape(bf16[768,2,16,32]{3,2,1,0:T(8,128)(2,1)} %bitcast.84) | data formatting | bytes 3145728
  78.6 5.0 %all-to-all-start.1 = ((bf16[4,2,98304]{2,1,0:T(2,128)(2,1)}), bf16[4,2,98304]{2,1,0:T(2,128)(2,1)S(1)}, u32[]{:S(2)}, u32[]{:S(2)}) async-start(bf16[4,2,98304]{2,1,0:T(2,128)(2,1)} %reshape.311), calls=%async_computation.1 | async-start | bytes 3145728 | tf_op jit(solution)/shard_map/all_to_all | solution.py:66
  84.3 34.6 %all-to-all-done.1 = bf16[4,2,98304]{2,1,0:T(2,128)(2,1)S(1)} async-done(((bf16[4,2,98304]{2,1,0:T(2,128)(2,1)}), bf16[4,2,98304]{2,1,0:T(2,128)(2,1)S(1)}, u32[]{:S(2)}, u32[]{:S(2)}) %all-to-all-start.1) | async-done | bytes 1572896 | tf_op jit(solution)/shard_map/all_to_all | solution.py:66
  118.8 4.6 %reshape.312 = bf16[768,2,16,32]{3,2,1,0:T(8,128)(2,1)} reshape(bf16[4,2,98304]{2,1,0:T(2,128)(2,1)S(1)} %all-to-all-done.1) | data formatting | bytes 3145728
  123.5 10.1 %copy.60 = bf16[32,4,192,2,16]{2,1,4,3,0:T(4,128)(2,1)S(1)} copy(bf16[32,4,192,2,16]{0,4,3,2,1:T(8,128)(2,1)} %bitcast.85) | data formatting | bytes 3145728 | tf_op jit(solution)/shard_map/all_to_all | solution.py:66
  134.1 9.1 %bitcast_convert_fusion = bf16[32,192,1536]{2,1,0:T(8,128)(2,1)} fusion(bf16[32,192,2,64]{1,3,2,0:T(8,128)(2,1)S(1)} %bitcast.86, bf16[1,64,1536]{2,1,0:T(8,128)(2,1)S(1)} %multiply_convert_fusion, bf16[1,64,1536]{2,1,0:T(8,128)(2,1)S(1)} %multiply_convert_fusion.1), kind=kOutput, calls=%fused_computation.4 | convolution fusion | flops 2425552896 | bytes 20840448 | tf_op jit(solution)/shard_map/lrcm,cmk->lrk/dot_general | solution.py:74
  143.2 35.2 %reshape.265 = bf16[32,2304,128]{2,1,0:T(8,128)(2,1)} reshape(bf16[32,192,1536]{2,1,0:T(8,128)(2,1)} %bitcast_convert_fusion) | data formatting | bytes 37748736 | tf_op jit(solution)/shard_map/reshape | solution.py:91
  178.4 20.7 %copy.52 = bf16[32,2304,128]{2,0,1:T(8,128)(2,1)} copy(bf16[32,2304,128]{2,1,0:T(8,128)(2,1)} %reshape.265) | data formatting | bytes 37748736 | tf_op jit(solution)/shard_map/reshape | solution.py:91
  199.1 7.1 %gather_fusion = bf16[96,32,128]{2,1,0:T(8,128)(2,1)S(1)} fusion(bf16[32,2304,128]{2,0,1:T(8,128)(2,1)} %copy.52, s32[1024]{0:T(1024)S(1)} %pad_clamp_fusion.1), kind=kCustom, calls=%fused_computation.2 | custom fusion | bytes 1573248 | tf_op jit(solution)/shard_map/jit(_take)/gather | solution.py:92
  206.2 1.1 select_bitcast_fusion
  207.3 3.5 all-to-all-start.2
  211.0 19.5 %all-to-all-done.2 = bf16[32,96,128]{2,0,1:T(8,128)(2,1)S(1)} async-done(((bf16[32,96,128]{2,0,1:T(8,128)(2,1)}), bf16[32,96,128]{2,0,1:T(8,128)(2,1)S(1)}, u32[]{:S(2)}, u32[]{:S(2)}) %all-to-all-start.2) | async-done | bytes 786464 | tf_op jit(solution)/shard_map/all_to_all | solution.py:93
  231.9 3.8 %collective-permute-start.2 = (bf16[32,128]{1,0:T(8,128)(2,1)S(1)}, bf16[32,128]{1,0:T(8,128)(2,1)S(1)}, u32[]{:S(2)}, u32[]{:S(2)}) collective-permute-start(bf16[32,128]{1,0:T(8,128)(2,1)S(1)} %get-tuple-element.12), channel_id=1, source_target_pairs={{4,0},{8,4},{12,8},{0,12},{5,1},{9,5},{13,9},{1,13},{6,2},{10,6},{... | collective-permute-start | bytes 24584 | tf_op jit(solution)/shard_map/ppermute | solution.py:36
  235.7 1.6 collective-permute-done.1
  237.9 43.6 %gather_fusion.2 = bf16[12288,32]{1,0:T(8,128)(2,1)} fusion(bf16[32,4352]{0,1:T(8,128)(2,1)S(1)} %copy.54, s32[12288]{0:T(1024)S(1)} %fusion.28), kind=kCustom, calls=%fused_computation.clone | custom fusion | bytes 1622016 | tf_op jit(solution)/shard_map/jit(_take)/gather | solution.py:114
  281.5 43.6 %gather_fusion.3 = bf16[12288,32]{1,0:T(8,128)(2,1)} fusion(bf16[32,4352]{0,1:T(8,128)(2,1)S(1)} %copy.54, s32[12288]{0:T(1024)S(1)} %fusion.29), kind=kCustom, calls=%fused_computation.1.clone | custom fusion | bytes 1622016 | tf_op jit(solution)/shard_map/jit(_take)/gather | solution.py:115
  325.1 12.1 %subtract_multiply_fusion = f32[32,12288]{0,1:T(8,128)} fusion(bf16[12288,32]{1,0:T(8,128)(2,1)} %gather_fusion.3, bf16[12288,32]{1,0:T(8,128)(2,1)} %gather_fusion.2, f32[12288]{0:T(1024)S(1)} %bitcast.96, pred[12288]{0:T(1024)(128)(4,1)S(1)} %get-tuple-element.17, pred[12288]{0:T(1024)(128)(4,1)S(1)} %get-tuple-element.18), kind=kLoop, calls=%fused_computation.13 | loop fusion | flops 2359296 | bytes 3219456 | tf_op jit(solution)/shard_map/mul | solution.py:113
  337.2 5.6 %copy.61 = f32[32,12288]{1,0:T(8,128)} copy(f32[32,12288]{0,1:T(8,128)} %subtract_multiply_fusion) | data formatting | bytes 3145728
  342.8 9.8 %reduce-scatter.4.cloned.1.call-done = f32[16,12288]{1,0:T(8,128)} async-done(((f32[32,12288]{1,0:T(8,128)}), f32[16,12288]{1,0:T(8,128)}) %reduce-scatter.4.cloned.1.call-update) | async-done | bytes 786448 | tf_op jit(solution)/shard_map/reduce_scatter | solution.py:117
  352.6 1.9 convert_element_type.53
  (48 shorter events, 6.1 us)
Async XLA Ops:
  6.5 224.5 %copy-start = (bf16[1,32,128,128]{3,2,1,0:T(8,128)(2,1)S(1)}, bf16[1,32,128,128]{3,2,1,0:T(8,128)(2,1)}, u32[]{:S(2)}) copy-start(bf16[1,32,128,128]{3,2,1,0:T(8,128)(2,1)} %param.13) | copy-start | bytes 3145732
  6.5 26.3 %collective-permute-start = (bf16[16,2,32,512]{3,2,1,0:T(8,128)(2,1)}, bf16[16,2,32,512]{3,2,1,0:T(8,128)(2,1)S(1)}, u32[]{:S(2)}, u32[]{:S(2)}) collective-permute-start(bf16[16,2,32,512]{3,2,1,0:T(8,128)(2,1)} %bitcast.91), channel_id=1, source_target_pairs={{0,2},{2,0},{1,3},{3,1},{4,6},{6,4},{5,7},{7,5},{8,10},{10,8},{9,1... | collective-permute-start | bytes 3145736 | tf_op jit(solution)/shard_map/ppermute | solution.py:17
  14.5 28.2 %copy-start.6 = (s32[32]{0:T(128)}, s32[32]{0:T(128)S(1)}, u32[]{:S(2)}) copy-start(s32[32]{0:T(128)S(1)} %convert_reduce_fusion) | copy-start | bytes 388
  16.1 16.8 %copy-start.1 = (bf16[16,384,512]{2,1,0:T(8,128)(2,1)S(1)}, bf16[16,384,512]{2,1,0:T(8,128)(2,1)}, u32[]{:S(2)}) copy-start(bf16[16,384,512]{2,1,0:T(8,128)(2,1)} %param.10) | copy-start | bytes 18874372
  39.1 22.6 %all-to-all-start = ((bf16[64,384,2,16]{1,2,3,0:T(2,128)(2,1)}), bf16[64,384,2,16]{1,2,3,0:T(2,128)(2,1)S(1)}, u32[]{:S(2)}, u32[]{:S(2)}) async-start(bf16[64,384,2,16]{1,2,3,0:T(2,128)(2,1)} %copy.47), calls=%async_computation | async-start | bytes 3145728 | tf_op jit(solution)/shard_map/all_to_all | solution.py:67
  78.6 5.0 %copy-start.5 = (f32[1,2,12288]{2,1,0:T(2,128)S(1)}, f32[1,2,12288]{2,1,0:T(2,128)}, u32[]{:S(2)}) copy-start(f32[1,2,12288]{2,1,0:T(2,128)} %param.15) | copy-start | bytes 294916
  78.6 40.2 %all-to-all-start.1 = ((bf16[4,2,98304]{2,1,0:T(2,128)(2,1)}), bf16[4,2,98304]{2,1,0:T(2,128)(2,1)S(1)}, u32[]{:S(2)}, u32[]{:S(2)}) async-start(bf16[4,2,98304]{2,1,0:T(2,128)(2,1)} %reshape.311), calls=%async_computation.1 | async-start | bytes 3145728 | tf_op jit(solution)/shard_map/all_to_all | solution.py:66
  199.1 11.7 %copy-start.7 = (s32[32]{0:T(128)S(1)}, s32[32]{0:T(128)}, u32[]{:S(2)}) copy-start(s32[32]{0:T(128)} %copy-done.6) | copy-start | bytes 388
  199.1 11.8 %copy-start.3 = (s32[1,1,12288]{2,1,0:T(1,128)S(1)}, s32[1,1,12288]{2,1,0:T(1,128)}, u32[]{:S(2)}) copy-start(s32[1,1,12288]{2,1,0:T(1,128)} %get-tuple-element.13) | copy-start | bytes 147460
  199.1 11.8 %copy-start.2 = (s32[1,1,12288]{2,1,0:T(1,128)S(1)}, s32[1,1,12288]{2,1,0:T(1,128)}, u32[]{:S(2)}) copy-start(s32[1,1,12288]{2,1,0:T(1,128)} %get-tuple-element.14) | copy-start | bytes 147460
  207.3 23.1 %all-to-all-start.2 = ((bf16[32,96,128]{2,0,1:T(8,128)(2,1)}), bf16[32,96,128]{2,0,1:T(8,128)(2,1)S(1)}, u32[]{:S(2)}, u32[]{:S(2)}) async-start(bf16[32,96,128]{2,0,1:T(8,128)(2,1)} %select_bitcast_fusion), calls=%async_computation.2 | async-start | bytes 1572864 | tf_op jit(solution)/shard_map/all_to_all | solution.py:93
  210.8 141.8 %reduce-scatter.4.cloned.1.call-start = ((), (), s32[]{:S(2)}) async-start(), calls=%async_computation.4 | async-start | bytes 2359296 | tf_op jit(solution)/shard_map/reduce_scatter | solution.py:117
  231.8 5.5 %collective-permute-start.1 = (bf16[32,128]{1,0:T(8,128)(2,1)S(1)}, bf16[32,128]{1,0:T(8,128)(2,1)S(1)}, u32[]{:S(2)}, u32[]{:S(2)}) collective-permute-start(bf16[32,128]{1,0:T(8,128)(2,1)S(1)} %get-tuple-element.11), channel_id=1, source_target_pairs={{0,4},{4,8},{8,12},{12,0},{1,5},{5,9},{9,13},{13,1},{2,6},{6,10},{... | collective-permute-start | bytes 24584 | tf_op jit(solution)/shard_map/ppermute | solution.py:34
  231.9 5.4 %collective-permute-start.2 = (bf16[32,128]{1,0:T(8,128)(2,1)S(1)}, bf16[32,128]{1,0:T(8,128)(2,1)S(1)}, u32[]{:S(2)}, u32[]{:S(2)}) collective-permute-start(bf16[32,128]{1,0:T(8,128)(2,1)S(1)} %get-tuple-element.12), channel_id=1, source_target_pairs={{4,0},{8,4},{12,8},{0,12},{5,1},{9,5},{13,9},{1,13},{6,2},{10,6},{... | collective-permute-start | bytes 24584 | tf_op jit(solution)/shard_map/ppermute | solution.py:36
  281.5 43.6 %copy-start.4 = (f32[1,1,12288]{2,1,0:T(1,128)S(1)}, f32[1,1,12288]{2,1,0:T(1,128)}, u32[]{:S(2)}) copy-start(f32[1,1,12288]{2,1,0:T(1,128)} %broadcast_select_fusion) | copy-start | bytes 147460
Sparse Core Ops, SparseCore 0:
  342.9 9.5 reduce-scatter.3
